TPU v7x, 32 devices: a whole 2x2x4 slice. The times are simulated.
32 devices in a mesh: survey: 2 (over x), sector: 16 (over z, y, core).
Axes of the slice: x: 2, y: 2, z: 4, core: 2. Of those that a mesh axis runs over, the one named last changes fastest.
Arguments:
- raw_pings: bfloat16 [32, 512, 2, 1024], P('survey', 'sector'), parts along dimension 0, may hold values from -6 to 6
- focus_matrix: bfloat16 [2, 2048, 512], replicated, may hold values from -0.25 to 0.25
- start_angle: int32 [32], P('survey'), parts along dimension 0, may hold values from 0 to 2047
- ping_count: int32 [32], P('survey'), parts along dimension 0, may hold values from 256 to 512, as said below
Outputs:
- coherence: float32 [32, 2048, 1024], P(('survey', 'sector')), parts along dimension 0
- interferogram: bfloat16 [32, 2, 2048, 1024], P(('survey', 'sector')), parts along dimension 0
There are 2 independent parts, one for each index of `survey`. A program takes and returns all parts, laid end to end along the dimension named above; an argument that names none is the same for every part. Nothing has to cross between parts.
Inputs may be any that keep to these rules, and one draw needn't show every extreme that they name: `ping_count`: every value lies between 256 and 512, and at least one sector holds all 512 pings.
All inputs are finite; a program needn't handle non-finite values.
Results may differ from a plain program's by a relative error of at most 0.0057.
Values may be sent and summed in bfloat16 or wider, within the bound.
No kernel may reach another device: no remote copies, remote signals or barrier semaphores. Data moves between devices by JAX's collectives and lax.ppermute only.
A program may use at most 192 MiB of HBM per device.

v0:
```python
import jax
import jax.numpy as jnp
from jax import lax
from jax.sharding import PartitionSpec as P

WIN = 9


def shifted(block, axis, distance):
    devices = range(lax.axis_size(axis))
    route = [((i - distance) % len(devices), i) for i in devices]
    return lax.ppermute(block, axis, route)


def focus_sector(raw, angle_step, valid_pings, stacked):
    pings_here = raw.shape[0]
    ranges_here = raw.shape[2]
    columns_count = stacked.shape[0] // 2
    ping_mask = (jnp.arange(pings_here, dtype=jnp.int32) < valid_pings).astype(jnp.bfloat16)
    masked = raw * ping_mask[:, None, None]
    product = jnp.dot(
        stacked, masked.reshape(pings_here, 2 * ranges_here), preferred_element_type=jnp.float32
    )
    product = product.reshape(2, columns_count, 2, ranges_here)
    real_part = product[0, :, 0] - product[1, :, 1]
    imag_part = product[0, :, 1] + product[1, :, 0]
    columns = jnp.arange(columns_count, dtype=jnp.int32)
    turn_index = angle_step * columns % columns_count
    phase_turn = 2.0 * jnp.pi / columns_count * turn_index.astype(jnp.float32)
    cosine = jnp.cos(phase_turn)[:, None]
    sine_part = jnp.sin(phase_turn)[:, None]
    mean_power = jnp.mean(real_part * real_part + imag_part * imag_part, axis=0)
    inverse_rms = lax.rsqrt(mean_power + 1e-06)
    turned_real = (real_part * cosine + imag_part * sine_part) * inverse_rms
    turned_imag = (imag_part * cosine - real_part * sine_part) * inverse_rms
    return jnp.stack([turned_real, turned_imag], axis=1).astype(jnp.bfloat16)


def window_sum(field, axis, span):
    half_span = span // 2
    length_axis = field.shape[axis]
    widths = [(0, 0)] * field.ndim
    widths[axis] = (half_span, half_span)
    padded = jnp.pad(field, widths)
    total = lax.slice_in_dim(padded, 0, length_axis, axis=axis)
    for offset in range(1, span):
        total = total + lax.slice_in_dim(padded, offset, offset + length_axis, axis=axis)
    return total


def compare(own_image, other_image, span):
    f_real = own_image[:, 0].astype(jnp.float32)
    f_imag = own_image[:, 1].astype(jnp.float32)
    g_real = other_image[:, 0].astype(jnp.float32)
    g_imag = other_image[:, 1].astype(jnp.float32)
    fields = jnp.stack(
        [
            f_real * g_real + f_imag * g_imag,
            f_imag * g_real - f_real * g_imag,
            f_real * f_real + f_imag * f_imag,
            g_real * g_real + g_imag * g_imag,
        ],
        axis=0,
    )
    looked = window_sum(window_sum(fields, 1, span), 2, span)
    magnitude = jnp.sqrt(looked[0] * looked[0] + looked[1] * looked[1])
    energy = jnp.sqrt(looked[2] * looked[3] + 1e-06)
    coherence = magnitude / energy
    interferogram = (looked[0:2] / float(span * span)).astype(jnp.bfloat16)
    return (coherence, interferogram)


def body(raw_pings, focus_matrix, start_angle, ping_count):
    stacked = focus_matrix.reshape(2 * focus_matrix.shape[1], focus_matrix.shape[2])
    position = lax.axis_index("sector")

    def prepare(pieces, sector):
        return focus_sector(pieces[0], start_angle[sector], ping_count[sector], stacked)[None]

    own_image = (lambda pieces: prepare(pieces, position))(
        lax.all_to_all(raw_pings, "sector", split_axis=0, concat_axis=1, tiled=True)
    )
    other_image = shifted(own_image, "sector", -1)
    coherence, interferogram = compare(own_image[0], other_image[0], WIN)
    return (coherence[None], interferogram[None])


def solution(mesh):
    return jax.shard_map(
        body,
        mesh=mesh,
        in_specs=(P("survey", "sector", None, None), P(), P("survey"), P("survey")),
        out_specs=(P(("survey", "sector"), None, None), P(("survey", "sector"), None, None, None)),
        check_vma=False,
    )
```

profile of v0, /device:TPU:0, one launch (start us, length us, event | category | flops | bytes accessed | tf_op | source)
XLA Modules:
  0.0 722.9 jit_solution(4973740520128592052)
XLA Ops:
  0.6 7.4 %all-to-all-start = ((bf16[16,32,2,1024]{3,2,1,0:T(2,128)(2,1)}), bf16[16,32,2,1024]{3,2,1,0:T(2,128)(2,1)S(1)}, u32[]{:S(2)}, u32[]{:S(2)}) async-start(bf16[16,32,2,1024]{3,2,1,0:T(2,128)(2,1)} %param.4), calls=%async_computation | async-start | bytes 4194304 | tf_op jit(solution)/shard_map/all_to_all | solution.py:81
  8.1 1.2 dynamic_slice.6
  9.3 1.2 dynamic_slice.7
  10.5 0.7 fusion.37
  11.2 0.7 fusion.38
  11.9 37.1 %all-to-all-done = bf16[16,32,2,1024]{3,2,1,0:T(2,128)(2,1)S(1)} async-done(((bf16[16,32,2,1024]{3,2,1,0:T(2,128)(2,1)}), bf16[16,32,2,1024]{3,2,1,0:T(2,128)(2,1)S(1)}, u32[]{:S(2)}, u32[]{:S(2)}) %all-to-all-start) | async-done | bytes 2097184 | tf_op jit(solution)/shard_map/all_to_all | solution.py:81
  49.0 1.9 broadcast_multiply_fusion
  50.9 0.6 copy.14
  51.5 17.5 %convolution_bitcast_fusion = f32[4096,2048]{0,1:T(8,128)} fusion(bf16[512,2048]{1,0:T(8,128)(2,1)S(1)} %bitcast.52, bf16[4096,512]{1,0:T(8,128)(2,1)} %bitcast.53), kind=kOutput, calls=%fused_computation.23 | convolution fusion | flops 8589934592 | bytes 39845888 | tf_op jit(solution)/shard_map/dot_general | solution.py:21
  69.0 42.6 %reshape.411 = f32[2,2048,2,1024]{1,0,3,2:T(2,128)} reshape(f32[4096,2048]{0,1:T(8,128)} %convolution_bitcast_fusion) | data formatting | bytes 67108864 | tf_op jit(solution)/shard_map/reshape | solution.py:24
  111.7 39.8 %fusion.42 = (f32[1,2048,1,1024]{1,0,3,2:T(1,128)}, f32[1,2048,1,1024]{1,0,3,2:T(1,128)}, f32[1,2048,1,1024]{1,0,3,2:T(1,128)}, f32[1,2048,1,1024]{1,0,3,2:T(1,128)}) fusion(f32[2,2048,2,1024]{1,0,3,2:T(2,128)} %reshape.411), kind=kLoop, calls=%fused_computation.80 | loop fusion | bytes 67108864 | tf_op jit(solution)/shard_map/slice | solution.py:25
  151.5 20.7 %copy.10 = f32[1,2048,1,1024]{3,1,2,0:T(8,128)} copy(f32[1,2048,1,1024]{1,0,3,2:T(1,128)} %get-tuple-element.10) | data formatting | bytes 16777216
  172.3 20.7 %copy.11 = f32[1,2048,1,1024]{3,1,2,0:T(8,128)} copy(f32[1,2048,1,1024]{1,0,3,2:T(1,128)} %get-tuple-element.8) | data formatting | bytes 16777216
  192.9 20.5 %copy.12 = f32[1,2048,1,1024]{3,1,2,0:T(8,128)} copy(f32[1,2048,1,1024]{1,0,3,2:T(1,128)} %get-tuple-element.9) | data formatting | bytes 16777216
  213.5 20.5 %copy.13 = f32[1,2048,1,1024]{3,1,2,0:T(8,128)} copy(f32[1,2048,1,1024]{1,0,3,2:T(1,128)} %get-tuple-element.11) | data formatting | bytes 16777216
  234.0 19.2 %add_reduce_fusion = (f32[1024]{0:T(1024)S(1)}, f32[1,2048,1,1024]{3,1,2,0:T(8,128)}, f32[1,2048,1,1024]{3,1,2,0:T(8,128)}) fusion(f32[1,2048,1,1024]{3,1,2,0:T(8,128)} %copy.12, f32[1,2048,1,1024]{3,1,2,0:T(8,128)} %copy.13, f32[1,2048,1,1024]{3,1,2,0:T(8,128)} %copy.10, f32[1,2048,1,1024]{3,1,2,0:T(8,128)} %copy.11), kind=kLoop, calls=%fused_computation.64 | loop fusion | flops 12581888 | bytes 50335744 | tf_op jit(solution)/shard_map/reduce_sum | solution.py:32
  253.3 8.6 %multiply_convert_fusion.1 = (bf16[1,2048,1,1024]{3,1,2,0:T(8,128)(2,1)S(1)}, bf16[1,2048,1,1024]{3,1,2,0:T(8,128)(2,1)}) fusion(f32[1,2048,1,1024]{3,1,2,0:T(8,128)} %get-tuple-element.6, f32[1,2048,1,1024]{3,1,2,0:T(8,128)} %get-tuple-element.7, f32[1024]{0:T(1024)S(1)} %add_rsqrt_fusion, f32[2048]{0:T(1024)S(1)} %get-tuple-element.17, ...), kind=kLoop, calls=%fused_computation.63 | loop fusion | flops 20971520 | bytes 25186304 | tf_op jit(solution)/shard_map/convert
  261.9 6.2 pad_maximum_fusion.1
  268.0 9.8 %collective-permute-start = (bf16[1,2048,2,1024]{3,1,2,0:T(8,128)(2,1)}, bf16[1,2048,2,1024]{3,1,2,0:T(8,128)(2,1)S(1)}, u32[]{:S(2)}, u32[]{:S(2)}) collective-permute-start(bf16[1,2048,2,1024]{3,1,2,0:T(8,128)(2,1)} %pad_maximum_fusion.1), channel_id=1, source_target_pairs={{1,0},{2,1},{3,2},{4,3},{5,4},{6,5},{7,6},{8,7},{9,8},{10,9},{11,1... | collective-permute-start | bytes 25165832 | tf_op jit(solution)/shard_map/ppermute | solution.py:12
  277.9 91.3 %collective-permute-done = bf16[1,2048,2,1024]{3,1,2,0:T(8,128)(2,1)S(1)} collective-permute-done((bf16[1,2048,2,1024]{3,1,2,0:T(8,128)(2,1)}, bf16[1,2048,2,1024]{3,1,2,0:T(8,128)(2,1)S(1)}, u32[]{:S(2)}, u32[]{:S(2)}) %collective-permute-start) | collective-permute-done | bytes 8388640 | tf_op jit(solution)/shard_map/ppermute | solution.py:12
  369.2 13.3 %fusion.14 = (f32[1,2048,1024]{2,1,0:T(8,128)}, bf16[2048,1,1024]{2,0,1:T(8,128)(2,1)S(1)}, bf16[2048,1,1024]{2,0,1:T(8,128)(2,1)}) fusion(bf16[2048,2,1024]{2,0,1:T(8,128)(2,1)S(1)} %bitcast.49, f32[1024]{0:T(1024)S(1)} %add_rsqrt_fusion, f32[2048]{0:T(1024)S(1)} %get-tuple-element.17, f32[1,2048,1,1024]{3,1,2,0:T(8,128)} %get-tuple-element.7, ...), kind=kLoop, calls=%fused_computation.37 | loop fusion | flops 35651584 | bytes 41963520 | tf_op jit(solution)/shard_map/add | solution.py:58
  382.5 11.1 %fusion.18 = (f32[1,2048,1024]{2,1,0:T(8,128)}, f32[1,2048,1024]{2,1,0:T(8,128)}, f32[1,2048,1024]{2,1,0:T(8,128)}) fusion(bf16[2048,1,1024]{2,0,1:T(8,128)(2,1)S(1)} %get-tuple-element.3, bf16[2048,1,1024]{2,0,1:T(8,128)(2,1)} %get-tuple-element.4, bf16[2048,2,1024]{2,0,1:T(8,128)(2,1)S(1)} %bitcast.50), kind=kLoop, calls=%fused_computation.41 | loop fusion | flops 27262976 | bytes 41943040 | tf_op jit(solution)/shard_map/sub | solution.py:59
  393.6 23.4 %pad_maximum_fusion = f32[4,2048,1024]{2,1,0:T(8,128)} fusion(f32[1,2048,1024]{2,1,0:T(8,128)} %get-tuple-element.15, f32[1,2048,1024]{2,1,0:T(8,128)} %get-tuple-element.16, f32[1,2048,1024]{2,1,0:T(8,128)} %get-tuple-element.14, f32[1,2048,1024]{2,1,0:T(8,128)} %get-tuple-element.2), kind=kLoop, calls=%fused_computation.16 | loop fusion | flops 25165824 | bytes 67108864 | tf_op jit(solution)/shard_map/stack | solution.py:56
  417.0 131.8 %slice_add_fusion = f32[4,2048,1024]{2,1,0:T(8,128)} fusion(f32[4,2048,1024]{2,1,0:T(8,128)} %pad_maximum_fusion), kind=kLoop, calls=%fused_computation.17 | loop fusion | flops 67108864 | bytes 67108864 | tf_op jit(solution)/shard_map/add | solution.py:47
  548.8 147.7 %fusion.7 = f32[4,2048,1024]{2,1,0:T(8,128)} fusion(f32[4,2048,1024]{2,1,0:T(8,128)} %slice_add_fusion), kind=kLoop, calls=%fused_computation.15 | loop fusion | flops 67108864 | bytes 67108864 | tf_op jit(solution)/shard_map/add | solution.py:47
  696.5 9.6 %fusion.19 = bf16[1,2,2048,1024]{3,2,1,0:T(8,128)(2,1)} fusion(f32[4,2048,1024]{2,1,0:T(8,128)} %fusion.7), kind=kLoop, calls=%fused_computation.42 | loop fusion | flops 8388608 | bytes 25165824 | tf_op jit(solution)/shard_map/broadcast_in_dim | solution.py:85
  706.1 16.7 %fusion.22 = f32[1,2048,1024]{2,1,0:T(8,128)} fusion(f32[4,2048,1024]{2,1,0:T(8,128)} %fusion.7), kind=kLoop, calls=%fused_computation.46 | loop fusion | flops 12582912 | bytes 41943040 | tf_op jit(solution)/shard_map/div | solution.py:68
  (1 shorter events, 0.0 us)
Async XLA Ops:
  0.6 48.4 %all-to-all-start = ((bf16[16,32,2,1024]{3,2,1,0:T(2,128)(2,1)}), bf16[16,32,2,1024]{3,2,1,0:T(2,128)(2,1)S(1)}, u32[]{:S(2)}, u32[]{:S(2)}) async-start(bf16[16,32,2,1024]{3,2,1,0:T(2,128)(2,1)} %param.4), calls=%async_computation | async-start | bytes 4194304 | tf_op jit(solution)/shard_map/all_to_all | solution.py:81
  268.0 101.1 %collective-permute-start = (bf16[1,2048,2,1024]{3,1,2,0:T(8,128)(2,1)}, bf16[1,2048,2,1024]{3,1,2,0:T(8,128)(2,1)S(1)}, u32[]{:S(2)}, u32[]{:S(2)}) collective-permute-start(bf16[1,2048,2,1024]{3,1,2,0:T(8,128)(2,1)} %pad_maximum_fusion.1), channel_id=1, source_target_pairs={{1,0},{2,1},{3,2},{4,3},{5,4},{6,5},{7,6},{8,7},{9,8},{10,9},{11,1... | collective-permute-start | bytes 25165832 | tf_op jit(solution)/shard_map/ppermute | solution.py:12
where the time goes:
time: 726 us; the launch traced here: 723 us
  other arithmetic  391 us (54%)
  local copies, waits for them, and re-layouts  168 us (23%)
  waiting for transfers between devices  128 us (18%)
  matrix products  17.5 us (2%)
  starting transfers between devices  17.3 us (2%)
    add x2, other arithmetic, window_sum(): total + lax.slice_in_dim(padded, offset, offset + length_axis, axis=axis)  280 us
    ppermute x1, waiting for transfers between devices, shifted(): return lax.ppermute(block, axis, route)  91.3 us
    unnamed x5, local copies, waits for them, and re-layouts  83.1 us
    reshape x1, local copies, waits for them, and re-layouts, focus_sector(): product = product.reshape(2, columns_count, 2, ranges_here)  42.6 us
    slice x1, local copies, waits for them, and re-layouts, focus_sector(): real_part = product[0, :, 0] - product[1, :, 1]  39.8 us
    all_to_all x1, waiting for transfers between devices, body(): lax.all_to_all(raw_pings, 'sector', split_axis=0, concat_axis=1, tiled=True)  37.1 us
    another operation x1, other arithmetic, compare(): jnp.stack([f_real * g_real + f_imag * g_imag, f_imag * g_real - f_real *...  23.4 us
    reduce_sum x1, other arithmetic, focus_sector(): mean_power = jnp.mean(real_part * real_part + imag_part * imag_part, axis=0)  19.2 us
  transfers between devices with their start and end apart: 2, of which 2 were waited for; matrix products, arithmetic and copies ran while one was open for 1% of the time, Pallas kernels for 0%

commit v1 on v0

--- a/solution.py
+++ b/solution.py
@@ -4,6 +4,29 @@
 from jax.sharding import PartitionSpec as P
 
 WIN = 9
+
+
+def cut_along(shard, dim, peers):
+    before, after = (shard.shape[:dim], shard.shape[dim + 1 :])
+    return jnp.moveaxis(shard.reshape(*before, peers, -1, *after), dim, 0)
+
+
+def joined_along(parts, dim):
+    parts = jnp.moveaxis(parts, 0, dim)
+    lengths = parts.shape
+    return parts.reshape(*lengths[:dim], lengths[dim] * lengths[dim + 1], *lengths[dim + 2 :])
+
+
+def sent_to_each(shard, axis, split_dim, concat_dim):
+    length, here = (lax.axis_size(axis), lax.axis_index(axis))
+    parts = cut_along(shard, split_dim, length)
+    out = parts
+    for step in range(1, length):
+        target, source = ((here + step) % length, (here - step) % length)
+        sent = lax.dynamic_index_in_dim(parts, target, 0)
+        received = lax.ppermute(sent, axis, [(i, (i + step) % length) for i in range(length)])
+        out = lax.dynamic_update_slice_in_dim(out, received, source, axis=0)
+    return joined_along(out, concat_dim)
 
 
 def shifted(block, axis, distance):
@@ -77,9 +100,7 @@
     def prepare(pieces, sector):
         return focus_sector(pieces[0], start_angle[sector], ping_count[sector], stacked)[None]
 
-    own_image = (lambda pieces: prepare(pieces, position))(
-        lax.all_to_all(raw_pings, "sector", split_axis=0, concat_axis=1, tiled=True)
-    )
+    own_image = (lambda pieces: prepare(pieces, position))(sent_to_each(raw_pings, "sector", 0, 1))
     other_image = shifted(own_image, "sector", -1)
     coherence, interferogram = compare(own_image[0], other_image[0], WIN)
     return (coherence[None], interferogram[None])

time: 726 us -> 737 us (1.015)
  waiting for transfers between devices: 128 us -> 105 us
  starting transfers between devices: 17.3 us -> 35.2 us
  local copies, waits for them, and re-layouts: 168 us -> 178 us
    all_to_all x1 -> x0, waiting for transfers between devices: 37.1 us -> none  [body(): lax.all_to_all(raw_pings, 'sector', split_axis=0, concat_axis=1, tiled=True)]
    ppermute x0 -> x15, starting transfers between devices: none -> 30.6 us  [sent_to_each(): lax.ppermute(sent, axis, [(i, (i + step) % length) for i in range(length)])]
    ppermute x0 -> x15, waiting for transfers between devices: none -> 13.4 us  [sent_to_each(): lax.ppermute(sent, axis, [(i, (i + step) % length) for i in range(length)])]
    all_to_all x1 -> x0, starting transfers between devices: 7.43 us -> none  [body(): lax.all_to_all(raw_pings, 'sector', split_axis=0, concat_axis=1, tiled=True)]
    unnamed x5 -> x8, local copies, waits for them, and re-layouts: 83.1 us -> 84.8 us
  transfers between devices with their start and end apart: 2 -> 16, of which waited for: 2 -> 4; matrix products, arithmetic and copies ran while one was open for 1% -> 1% of each run, Pallas kernels for 0% -> 0%
where the time goes in v1:
time: 737 us; the launch traced here: 727 us
  other arithmetic  391 us (53%)
  local copies, waits for them, and re-layouts  178 us (24%)
  waiting for transfers between devices  105 us (14%)
  starting transfers between devices  35.2 us (5%)
  matrix products  18 us (2%)
    add x2, other arithmetic, window_sum(): total + lax.slice_in_dim(padded, offset, offset + length_axis, axis=axis)  278 us
    ppermute x1, waiting for transfers between devices, shifted(): return lax.ppermute(block, axis, route)  91.3 us
    unnamed x8, local copies, waits for them, and re-layouts  84.8 us
    reshape x1, local copies, waits for them, and re-layouts, focus_sector(): product = product.reshape(2, columns_count, 2, ranges_here)  42.6 us
    slice x1, local copies, waits for them, and re-layouts, focus_sector(): real_part = product[0, :, 0] - product[1, :, 1]  39.7 us
    ppermute x15, starting transfers between devices, sent_to_each(): lax.ppermute(sent, axis, [(i, (i + step) % length) for i in range(length)])  30.6 us
    another operation x1, other arithmetic, compare(): jnp.stack([f_real * g_real + f_imag * g_imag, f_imag * g_real - f_real *...  23.5 us
    reduce_sum x1, other arithmetic, focus_sector(): mean_power = jnp.mean(real_part * real_part + imag_part * imag_part, axis=0)  19.1 us
  transfers between devices with their start and end apart: 16, of which 4 were waited for; matrix products, arithmetic and copies ran while one was open for 1% of the time, Pallas kernels for 0%

profile of v1, /device:TPU:0, one launch (start us, length us, event | category | flops | bytes accessed | tf_op | source)
XLA Modules:
  0.0 727.5 jit_solution(1112271260539730422)
XLA Ops:
  0.6 1.6 copy.31
  2.2 2.5 dynamic-slice_bitcast_fusion
  5.3 2.5 collective-permute-start.1
  7.8 2.5 collective-permute-start.2
  10.3 1.6 collective-permute-start.3
  18.0 4.4 collective-permute-start.6
  26.1 10.9 %collective-permute-done.4 = bf16[1,1,32,2,1024]{4,3,2,0,1:T(2,128)(2,1)} collective-permute-done((bf16[1,1,32,2,1024]{4,3,2,0,1:T(2,128)(2,1)S(1)}, bf16[1,1,32,2,1024]{4,3,2,0,1:T(2,128)(2,1)}, u32[]{:S(2)}, u32[]{:S(2)}) %collective-permute-start.4) | collective-permute-done | bytes 131104 | tf_op jit(solution)/shard_map/ppermute | solution.py:27
  38.0 3.0 collective-permute-start.10
  41.1 5.3 collective-permute-start.11
  47.8 4.7 collective-permute-start.13
  52.6 2.9 collective-permute-start.14
  56.0 2.4 collective-permute-done.13
  58.8 2.6 broadcast_multiply_fusion
  62.0 18.0 %convolution_bitcast_fusion = f32[4096,2048]{0,1:T(8,128)} fusion(bf16[512,2048]{1,0:T(8,128)(2,1)S(1)} %bitcast.85, bf16[4096,512]{1,0:T(8,128)(2,1)} %bitcast.86), kind=kOutput, calls=%fused_computation.23 | convolution fusion | flops 8589934592 | bytes 39845888 | tf_op jit(solution)/shard_map/dot_general | solution.py:44
  80.0 42.6 %reshape.425 = f32[2,2048,2,1024]{1,0,3,2:T(2,128)} reshape(f32[4096,2048]{0,1:T(8,128)} %convolution_bitcast_fusion) | data formatting | bytes 67108864 | tf_op jit(solution)/shard_map/reshape | solution.py:47
  122.6 39.7 %fusion.42 = (f32[1,2048,1,1024]{1,0,3,2:T(1,128)}, f32[1,2048,1,1024]{1,0,3,2:T(1,128)}, f32[1,2048,1,1024]{1,0,3,2:T(1,128)}, f32[1,2048,1,1024]{1,0,3,2:T(1,128)}) fusion(f32[2,2048,2,1024]{1,0,3,2:T(2,128)} %reshape.425), kind=kLoop, calls=%fused_computation.110 | loop fusion | bytes 67108864 | tf_op jit(solution)/shard_map/slice | solution.py:48
  162.4 20.8 %copy.10 = f32[1,2048,1,1024]{3,1,2,0:T(8,128)} copy(f32[1,2048,1,1024]{1,0,3,2:T(1,128)} %get-tuple-element.10) | data formatting | bytes 16777216
  183.2 20.7 %copy.11 = f32[1,2048,1,1024]{3,1,2,0:T(8,128)} copy(f32[1,2048,1,1024]{1,0,3,2:T(1,128)} %get-tuple-element.8) | data formatting | bytes 16777216
  203.9 20.5 %copy.12 = f32[1,2048,1,1024]{3,1,2,0:T(8,128)} copy(f32[1,2048,1,1024]{1,0,3,2:T(1,128)} %get-tuple-element.9) | data formatting | bytes 16777216
  224.4 20.5 %copy.13 = f32[1,2048,1,1024]{3,1,2,0:T(8,128)} copy(f32[1,2048,1,1024]{1,0,3,2:T(1,128)} %get-tuple-element.11) | data formatting | bytes 16777216
  245.0 19.1 %add_reduce_fusion = (f32[1024]{0:T(1024)S(1)}, f32[1,2048,1,1024]{3,1,2,0:T(8,128)}, f32[1,2048,1,1024]{3,1,2,0:T(8,128)}) fusion(f32[1,2048,1,1024]{3,1,2,0:T(8,128)} %copy.12, f32[1,2048,1,1024]{3,1,2,0:T(8,128)} %copy.13, f32[1,2048,1,1024]{3,1,2,0:T(8,128)} %copy.10, f32[1,2048,1,1024]{3,1,2,0:T(8,128)} %copy.11), kind=kLoop, calls=%fused_computation.64 | loop fusion | flops 12581888 | bytes 50335744 | tf_op jit(solution)/shard_map/reduce_sum | solution.py:55
  264.1 8.7 %multiply_convert_fusion.1 = (bf16[1,2048,1,1024]{3,1,2,0:T(8,128)(2,1)S(1)}, bf16[1,2048,1,1024]{3,1,2,0:T(8,128)(2,1)}) fusion(f32[1,2048,1,1024]{3,1,2,0:T(8,128)} %get-tuple-element.6, f32[1,2048,1,1024]{3,1,2,0:T(8,128)} %get-tuple-element.7, f32[1024]{0:T(1024)S(1)} %add_rsqrt_fusion, f32[2048]{0:T(1024)S(1)} %get-tuple-element.32, ...), kind=kLoop, calls=%fused_computation.63 | loop fusion | flops 20971520 | bytes 25186304 | tf_op jit(solution)/shard_map/convert
  272.8 6.2 pad_maximum_fusion.1
  279.0 4.6 collective-permute-start.15
  283.6 91.3 %collective-permute-done.15 = bf16[1,2048,2,1024]{3,1,2,0:T(8,128)(2,1)S(1)} collective-permute-done((bf16[1,2048,2,1024]{3,1,2,0:T(8,128)(2,1)}, bf16[1,2048,2,1024]{3,1,2,0:T(8,128)(2,1)S(1)}, u32[]{:S(2)}, u32[]{:S(2)}) %collective-permute-start.15) | collective-permute-done | bytes 8388640 | tf_op jit(solution)/shard_map/ppermute | solution.py:35
  374.9 13.3 %fusion.14 = (f32[1,2048,1024]{2,1,0:T(8,128)}, bf16[2048,1,1024]{2,0,1:T(8,128)(2,1)S(1)}, bf16[2048,1,1024]{2,0,1:T(8,128)(2,1)}) fusion(bf16[2048,2,1024]{2,0,1:T(8,128)(2,1)S(1)} %bitcast.81, f32[1024]{0:T(1024)S(1)} %add_rsqrt_fusion, f32[2048]{0:T(1024)S(1)} %get-tuple-element.32, f32[1,2048,1,1024]{3,1,2,0:T(8,128)} %get-tuple-element.7, ...), kind=kLoop, calls=%fused_computation.37 | loop fusion | flops 35651584 | bytes 41963520 | tf_op jit(solution)/shard_map/add | solution.py:81
  388.2 11.1 %fusion.18 = (f32[1,2048,1024]{2,1,0:T(8,128)}, f32[1,2048,1024]{2,1,0:T(8,128)}, f32[1,2048,1024]{2,1,0:T(8,128)}) fusion(bf16[2048,1,1024]{2,0,1:T(8,128)(2,1)S(1)} %get-tuple-element.3, bf16[2048,1,1024]{2,0,1:T(8,128)(2,1)} %get-tuple-element.4, bf16[2048,2,1024]{2,0,1:T(8,128)(2,1)S(1)} %bitcast.82), kind=kLoop, calls=%fused_computation.41 | loop fusion | flops 27262976 | bytes 41943040 | tf_op jit(solution)/shard_map/sub | solution.py:82
  399.3 23.5 %pad_maximum_fusion = f32[4,2048,1024]{2,1,0:T(8,128)} fusion(f32[1,2048,1024]{2,1,0:T(8,128)} %get-tuple-element.15, f32[1,2048,1024]{2,1,0:T(8,128)} %get-tuple-element.16, f32[1,2048,1024]{2,1,0:T(8,128)} %get-tuple-element.14, f32[1,2048,1024]{2,1,0:T(8,128)} %get-tuple-element.2), kind=kLoop, calls=%fused_computation.16 | loop fusion | flops 25165824 | bytes 67108864 | tf_op jit(solution)/shard_map/stack | solution.py:79
  422.8 131.1 %slice_add_fusion = f32[4,2048,1024]{2,1,0:T(8,128)} fusion(f32[4,2048,1024]{2,1,0:T(8,128)} %pad_maximum_fusion), kind=kLoop, calls=%fused_computation.17 | loop fusion | flops 67108864 | bytes 67108864 | tf_op jit(solution)/shard_map/add | solution.py:70
  553.9 147.0 %fusion.7 = f32[4,2048,1024]{2,1,0:T(8,128)} fusion(f32[4,2048,1024]{2,1,0:T(8,128)} %slice_add_fusion), kind=kLoop, calls=%fused_computation.15 | loop fusion | flops 67108864 | bytes 67108864 | tf_op jit(solution)/shard_map/add | solution.py:70
  700.9 9.6 %fusion.19 = bf16[1,2,2048,1024]{3,2,1,0:T(8,128)(2,1)} fusion(f32[4,2048,1024]{2,1,0:T(8,128)} %fusion.7), kind=kLoop, calls=%fused_computation.42 | loop fusion | flops 8388608 | bytes 25165824 | tf_op jit(solution)/shard_map/broadcast_in_dim | solution.py:106
  710.5 16.7 %fusion.22 = f32[1,2048,1024]{2,1,0:T(8,128)} fusion(f32[4,2048,1024]{2,1,0:T(8,128)} %fusion.7), kind=kLoop, calls=%fused_computation.46 | loop fusion | flops 12582912 | bytes 41943040 | tf_op jit(solution)/shard_map/div | solution.py:91
  (43 shorter events, 14.4 us)
Async XLA Ops:
  0.6 11.3 %copy-start = (s32[16]{0:T(128)S(1)}, s32[16]{0:T(128)}, u32[]{:S(2)}) copy-start(s32[16]{0:T(128)} %param.6) | copy-start | bytes 196
  4.8 11.0 %collective-permute-start = (bf16[1,1,32,2,1024]{4,3,2,0,1:T(2,128)(2,1)}, bf16[1,1,32,2,1024]{4,3,2,0,1:T(2,128)(2,1)}, u32[]{:S(2)}, u32[]{:S(2)}) collective-permute-start(bf16[1,1,32,2,1024]{4,3,2,0,1:T(2,128)(2,1)} %get-tuple-element.30), channel_id=1, source_target_pairs={{0,1},{1,2},{2,3},{3,4},{4,5},{5,6},{6,7},{7,8},{8,9},{9,10},{10,1... | collective-permute-start | bytes 393224 | tf_op jit(solution)/shard_map/ppermute | solution.py:27
  5.3 12.7 %collective-permute-start.1 = (bf16[1,1,32,2,1024]{4,3,2,0,1:T(2,128)(2,1)}, bf16[1,1,32,2,1024]{4,3,2,0,1:T(2,128)(2,1)}, u32[]{:S(2)}, u32[]{:S(2)}) collective-permute-start(bf16[1,1,32,2,1024]{4,3,2,0,1:T(2,128)(2,1)} %get-tuple-element.29), channel_id=1, source_target_pairs={{0,2},{1,3},{2,4},{3,5},{4,6},{5,7},{6,8},{7,9},{8,10},{9,11},{10,... | collective-permute-start | bytes 393224 | tf_op jit(solution)/shard_map/ppermute | solution.py:27
  7.8 15.6 %collective-permute-start.2 = (bf16[1,1,32,2,1024]{4,3,2,0,1:T(2,128)(2,1)}, bf16[1,1,32,2,1024]{4,3,2,0,1:T(2,128)(2,1)}, u32[]{:S(2)}, u32[]{:S(2)}) collective-permute-start(bf16[1,1,32,2,1024]{4,3,2,0,1:T(2,128)(2,1)} %get-tuple-element.28), channel_id=1, source_target_pairs={{0,3},{1,4},{2,5},{3,6},{4,7},{5,8},{6,9},{7,10},{8,11},{9,12},{10... | collective-permute-start | bytes 393224 | tf_op jit(solution)/shard_map/ppermute | solution.py:27
  10.3 14.6 %collective-permute-start.3 = (bf16[1,1,32,2,1024]{4,3,2,0,1:T(2,128)(2,1)}, bf16[1,1,32,2,1024]{4,3,2,0,1:T(2,128)(2,1)}, u32[]{:S(2)}, u32[]{:S(2)}) collective-permute-start(bf16[1,1,32,2,1024]{4,3,2,0,1:T(2,128)(2,1)} %get-tuple-element.27), channel_id=1, source_target_pairs={{0,4},{1,5},{2,6},{3,7},{4,8},{5,9},{6,10},{7,11},{8,12},{9,13},{1... | collective-permute-start | bytes 393224 | tf_op jit(solution)/shard_map/ppermute | solution.py:27
  11.8 25.2 %collective-permute-start.4 = (bf16[1,1,32,2,1024]{4,3,2,0,1:T(2,128)(2,1)S(1)}, bf16[1,1,32,2,1024]{4,3,2,0,1:T(2,128)(2,1)}, u32[]{:S(2)}, u32[]{:S(2)}) collective-permute-start(bf16[1,1,32,2,1024]{4,3,2,0,1:T(2,128)(2,1)S(1)} %get-tuple-element.26), channel_id=1, source_target_pairs={{0,5},{1,6},{2,7},{3,8},{4,9},{5,10},{6,11},{7,12},{8,13},{9,14},{... | collective-permute-start | bytes 393224 | tf_op jit(solution)/shard_map/ppermute | solution.py:27
  15.8 22.2 %collective-permute-start.5 = (bf16[1,1,32,2,1024]{4,3,2,0,1:T(2,128)(2,1)S(1)}, bf16[1,1,32,2,1024]{4,3,2,0,1:T(2,128)(2,1)S(1)}, u32[]{:S(2)}, u32[]{:S(2)}) collective-permute-start(bf16[1,1,32,2,1024]{4,3,2,0,1:T(2,128)(2,1)S(1)} %get-tuple-element.25), channel_id=1, source_target_pairs={{0,6},{1,7},{2,8},{3,9},{4,10},{5,11},{6,12},{7,13},{8,14},{9,15},... | collective-permute-start | bytes 393224 | tf_op jit(solution)/shard_map/ppermute | solution.py:27
  18.0 23.1 %collective-permute-start.6 = (bf16[1,1,32,2,1024]{4,3,2,0,1:T(2,128)(2,1)S(1)}, bf16[1,1,32,2,1024]{4,3,2,0,1:T(2,128)(2,1)S(1)}, u32[]{:S(2)}, u32[]{:S(2)}) collective-permute-start(bf16[1,1,32,2,1024]{4,3,2,0,1:T(2,128)(2,1)S(1)} %get-tuple-element.24), channel_id=1, source_target_pairs={{0,7},{1,8},{2,9},{3,10},{4,11},{5,12},{6,13},{7,14},{8,15},{9,0},... | collective-permute-start | bytes 393224 | tf_op jit(solution)/shard_map/ppermute | solution.py:27
  23.4 23.1 %collective-permute-start.7 = (bf16[1,1,32,2,1024]{4,3,2,0,1:T(2,128)(2,1)S(1)}, bf16[1,1,32,2,1024]{4,3,2,0,1:T(2,128)(2,1)S(1)}, u32[]{:S(2)}, u32[]{:S(2)}) collective-permute-start(bf16[1,1,32,2,1024]{4,3,2,0,1:T(2,128)(2,1)S(1)} %get-tuple-element.23), channel_id=1, source_target_pairs={{0,8},{1,9},{2,10},{3,11},{4,12},{5,13},{6,14},{7,15},{8,0},{9,1},... | collective-permute-start | bytes 393224 | tf_op jit(solution)/shard_map/ppermute | solution.py:27
  24.8 23.0 %collective-permute-start.8 = (bf16[1,1,32,2,1024]{4,3,2,0,1:T(2,128)(2,1)S(1)}, bf16[1,1,32,2,1024]{4,3,2,0,1:T(2,128)(2,1)S(1)}, u32[]{:S(2)}, u32[]{:S(2)}) collective-permute-start(bf16[1,1,32,2,1024]{4,3,2,0,1:T(2,128)(2,1)S(1)} %get-tuple-element.22), channel_id=1, source_target_pairs={{0,9},{1,10},{2,11},{3,12},{4,13},{5,14},{6,15},{7,0},{8,1},{9,2},... | collective-permute-start | bytes 393224 | tf_op jit(solution)/shard_map/ppermute | solution.py:27
  37.0 15.6 %collective-permute-start.9 = (bf16[1,1,32,2,1024]{4,3,2,0,1:T(2,128)(2,1)S(1)}, bf16[1,1,32,2,1024]{4,3,2,0,1:T(2,128)(2,1)S(1)}, u32[]{:S(2)}, u32[]{:S(2)}) collective-permute-start(bf16[1,1,32,2,1024]{4,3,2,0,1:T(2,128)(2,1)S(1)} %get-tuple-element.21), channel_id=1, source_target_pairs={{0,10},{1,11},{2,12},{3,13},{4,14},{5,15},{6,0},{7,1},{8,2},{9,3},... | collective-permute-start | bytes 393224 | tf_op jit(solution)/shard_map/ppermute | solution.py:27
  38.0 17.7 %collective-permute-start.10 = (bf16[1,1,32,2,1024]{4,3,2,0,1:T(2,128)(2,1)S(1)}, bf16[1,1,32,2,1024]{4,3,2,0,1:T(2,128)(2,1)S(1)}, u32[]{:S(2)}, u32[]{:S(2)}) collective-permute-start(bf16[1,1,32,2,1024]{4,3,2,0,1:T(2,128)(2,1)S(1)} %get-tuple-element.20), channel_id=1, source_target_pairs={{0,11},{1,12},{2,13},{3,14},{4,15},{5,0},{6,1},{7,2},{8,3},{9,4},{... | collective-permute-start | bytes 393224 | tf_op jit(solution)/shard_map/ppermute | solution.py:27
  41.1 14.7 %collective-permute-start.11 = (bf16[1,1,32,2,1024]{4,3,2,0,1:T(2,128)(2,1)S(1)}, bf16[1,1,32,2,1024]{4,3,2,0,1:T(2,128)(2,1)S(1)}, u32[]{:S(2)}, u32[]{:S(2)}) collective-permute-start(bf16[1,1,32,2,1024]{4,3,2,0,1:T(2,128)(2,1)S(1)} %get-tuple-element.19), channel_id=1, source_target_pairs={{0,12},{1,13},{2,14},{3,15},{4,0},{5,1},{6,2},{7,3},{8,4},{9,5},{1... | collective-permute-start | bytes 393224 | tf_op jit(solution)/shard_map/ppermute | solution.py:27
  46.5 9.4 %collective-permute-start.12 = (bf16[1,1,32,2,1024]{4,3,2,0,1:T(2,128)(2,1)S(1)}, bf16[1,1,32,2,1024]{4,3,2,0,1:T(2,128)(2,1)S(1)}, u32[]{:S(2)}, u32[]{:S(2)}) collective-permute-start(bf16[1,1,32,2,1024]{4,3,2,0,1:T(2,128)(2,1)S(1)} %get-tuple-element.18), channel_id=1, source_target_pairs={{0,13},{1,14},{2,15},{3,0},{4,1},{5,2},{6,3},{7,4},{8,5},{9,6},{10... | collective-permute-start | bytes 393224 | tf_op jit(solution)/shard_map/ppermute | solution.py:27
  47.8 10.7 %collective-permute-start.13 = (bf16[1,1,32,2,1024]{4,3,2,0,1:T(2,128)(2,1)S(1)}, bf16[1,1,32,2,1024]{4,3,2,0,1:T(2,128)(2,1)S(1)}, u32[]{:S(2)}, u32[]{:S(2)}) collective-permute-start(bf16[1,1,32,2,1024]{4,3,2,0,1:T(2,128)(2,1)S(1)} %get-tuple-element.31), channel_id=1, source_target_pairs={{0,14},{1,15},{2,0},{3,1},{4,2},{5,3},{6,4},{7,5},{8,6},{9,7},{10,... | collective-permute-start | bytes 393224 | tf_op jit(solution)/shard_map/ppermute | solution.py:27
  52.6 6.1 collective-permute-start.14
  279.0 95.9 %collective-permute-start.15 = (bf16[1,2048,2,1024]{3,1,2,0:T(8,128)(2,1)}, bf16[1,2048,2,1024]{3,1,2,0:T(8,128)(2,1)S(1)}, u32[]{:S(2)}, u32[]{:S(2)}) collective-permute-start(bf16[1,2048,2,1024]{3,1,2,0:T(8,128)(2,1)} %pad_maximum_fusion.1), channel_id=1, source_target_pairs={{1,0},{2,1},{3,2},{4,3},{5,4},{6,5},{7,6},{8,7},{9,8},{10,9},{11,1... | collective-permute-start | bytes 25165832 | tf_op jit(solution)/shard_map/ppermute | solution.py:35
